TPU v7x, 512 devices: a whole 4x4x16 slice. The times are simulated.
512 devices in a mesh: energy: 32 (over z, core), seg: 16 (over y, x).
Axes of the slice: x: 4, y: 4, z: 16, core: 2. Of those that a mesh axis runs over, the one named last changes fastest.
Arguments:
- energies: float32 [32], P('energy'), may hold values from -2 to 2
- h_blocks: float32 [16, 4, 64, 128], P('seg'), as said below
- couplings: float32 [16, 4, 64, 128], P('seg')
- shift_real: float32 [32, 16, 256], P('energy', 'seg'), may hold values from -0.625 to 0.625
- shift_rate: float32 [32, 16, 256], P('energy', 'seg'), may hold values from 0.005 to 0.05
- screened: float32 [8, 16, 4, 64, 128], P(None, 'seg'), may hold values from -3 to 3
- sources: int32 [32, 8], P('energy'), may hold values from 0 to 31, as said below
- counts: int32 [16], P('seg'), may hold values from 1 to 4, 32 in all
Outputs:
- sigma_new: float32 [32, 16, 4, 64, 128], P('energy', 'seg')
Inputs may be any that keep to these rules, and one draw needn't show every extreme that they name: `h_blocks`: each diagonal block is Hermitian: its real part symmetric, its imaginary part antisymmetric. The counts sum to 32; some segment holds exactly 4 blocks. For every group of 1 consecutive energies starting at a multiple of 1, its 8 sources lie at most 1 in any one such group, and exactly 1 in some group.
All inputs are finite; a program needn't handle non-finite values.
Results may differ from a plain program's by a relative error of at most 0.0029.
Values may be sent and summed in bfloat16 or wider, within the bound.
A program may use at most 64 MiB of HBM per device.

v0:
```python
import jax
import jax.numpy as jnp
from jax import lax
from jax.sharding import PartitionSpec as P

broadening = 0.02


def carried_in(part, axis, combine, identity, reverse):
    count = lax.axis_size(axis)
    place = lax.axis_index(axis)
    ahead = count - 1 - place if reverse else place
    gathered = jax.tree.map(lambda a: lax.all_gather(a, axis), part)
    state = jax.tree.map(lambda a, e: jnp.zeros_like(a) + jnp.asarray(e, a.dtype), part, identity)

    def one(turn, state):
        source = count - 1 - turn if reverse else turn
        return combine(
            state, jax.tree.map(lambda a: lax.dynamic_index_in_dim(a, source, 0, False), gathered)
        )

    return lax.fori_loop(0, ahead, one, state)


def expand(matrix):
    order = matrix.shape[-2]
    real_part = matrix[..., :order]
    imag_part = matrix[..., order:]
    return jnp.concatenate(
        [jnp.concatenate([real_part, imag_part], -1), jnp.concatenate([-imag_part, real_part], -1)],
        -2,
    )


def complex_product(matrix, other):
    return jnp.matmul(matrix, expand(other), precision=lax.Precision.HIGHEST)


def adjoint(matrix):
    order = matrix.shape[-2]
    return jnp.concatenate(
        [jnp.swapaxes(matrix[..., :order], -1, -2), -jnp.swapaxes(matrix[..., order:], -1, -2)], -1
    )


def complex_inverse(matrix):
    order = matrix.shape[-2]
    real_part = matrix[..., :order]
    imag_part = matrix[..., order:]
    real_form = jnp.concatenate(
        [jnp.concatenate([real_part, -imag_part], -1), jnp.concatenate([imag_part, real_part], -1)],
        -2,
    )
    flipped = jnp.swapaxes(real_form, -1, -2)
    normal = jnp.matmul(flipped, real_form, precision=lax.Precision.HIGHEST)
    factor = jnp.linalg.cholesky(normal)
    middle = jax.scipy.linalg.solve_triangular(factor, flipped[..., :order], lower=True)
    solved = jax.scipy.linalg.solve_triangular(factor, middle, lower=True, trans=1)
    return jnp.concatenate([solved[..., :order, :], solved[..., order:, :]], -1)


def unit_block(order):
    return jnp.concatenate(
        [jnp.eye(order, dtype=jnp.float32), jnp.zeros((order, order), jnp.float32)], -1
    )


def entry_product(green, weight):
    order = green.shape[-2]
    green_re = green[..., :order]
    green_im = green[..., order:]
    weight_re = weight[..., :order]
    weight_im = weight[..., order:]
    return jnp.concatenate(
        [green_re * weight_re - green_im * weight_im, green_re * weight_im + green_im * weight_re],
        -1,
    )


def build_blocks(energies, hams, shift_real, shift_rate):
    slots, order = (hams.shape[0], hams.shape[1])
    batch = energies.shape[0]
    identity = jnp.eye(order, dtype=jnp.float32)
    shifts = shift_real.reshape(batch, slots, order)
    rates = shift_rate.reshape(batch, slots, order)
    real_part = (
        energies[:, None, None, None] * identity
        - hams[None, :, :, :order]
        - shifts[..., :, None] * identity
    )
    imag_part = broadening * identity - hams[None, :, :, order:] + rates[..., :, None] * identity
    return jnp.concatenate([real_part, imag_part], -1)


def summary_step(diag_block, link_block, state):
    head_block, upper_block, lower_block, last_block = state
    back_link = adjoint(link_block)
    fresh_block = complex_inverse(
        diag_block - complex_product(complex_product(back_link, last_block), link_block)
    )
    left_part = complex_product(upper_block, link_block)
    right_part = complex_product(back_link, lower_block)
    new_upper = complex_product(left_part, fresh_block)
    new_lower = complex_product(fresh_block, right_part)
    new_head = head_block + complex_product(new_upper, right_part)
    return (new_head, new_upper, new_lower, fresh_block)


def summary_masked(diag_a, links, used_blocks):
    slots = diag_a.shape[1]
    last_block = complex_inverse(diag_a[:, 0])
    state = (last_block, last_block, last_block, last_block)
    for k in range(1, slots):
        updated = summary_step(diag_a[:, k], links[k], state)
        live = k < used_blocks
        state = tuple(
            (jnp.where(live, new_item, old_item) for new_item, old_item in zip(updated, state))
        )
    return state


def pick_blocks(flag, first_item, second_item):
    return jnp.where(flag[..., None, None] > 0.5, first_item, second_item)


def join_segments(left_group, right_group):
    a, b, c, d, entry_a, flag_a = left_group
    p, q, r, s, link_v, flag_b = right_group
    back_v = adjoint(link_v)
    order = a.shape[-2]
    cross_term = complex_product(complex_product(back_v, d), link_v)
    resolvent = complex_inverse(unit_block(order) - complex_product(p, cross_term))
    res_first = complex_product(resolvent, p)
    res_upper = complex_product(resolvent, q)
    d_link = complex_product(d, link_v)
    back_c = complex_product(back_v, c)
    b_link = complex_product(b, link_v)
    head_block = a + complex_product(complex_product(b_link, res_first), back_c)
    upper_block = complex_product(b_link, res_upper)
    k_lower = c + complex_product(complex_product(d_link, res_first), back_c)
    lower_block = complex_product(r, complex_product(back_v, k_lower))
    last_block = s + complex_product(complex_product(r, cross_term), res_upper)
    joined = (head_block, upper_block, lower_block, last_block, entry_a)
    result = tuple(
        (
            pick_blocks(flag_a, rb, pick_blocks(flag_b, lb, jb))
            for lb, rb, jb in zip(left_group[:5], right_group[:5], joined)
        )
    )
    return result + (flag_a * flag_b,)


def join_reversed(earlier, later):
    return join_segments(later, earlier)


def greens_masked(diag_a, links, used_blocks, previous, sig_right):
    slots = diag_a.shape[1]
    forward_blocks = []
    for k in range(slots):
        link_block = links[k]
        inner_block = (
            diag_a[:, k]
            - complex_product(complex_product(adjoint(link_block), previous), link_block)
            - jnp.where(k == used_blocks - 1, sig_right, 0.0)
        )
        fresh_block = complex_inverse(inner_block)
        forward_blocks.append(fresh_block)
        previous = fresh_block
    greens = list(forward_blocks)
    for k in range(slots - 2, -1, -1):
        link_block = links[k + 1]
        spread = complex_product(forward_blocks[k], link_block)
        updated = forward_blocks[k] + complex_product(
            complex_product(spread, greens[k + 1]),
            complex_product(adjoint(link_block), forward_blocks[k]),
        )
        greens[k] = jnp.where(k <= used_blocks - 2, updated, forward_blocks[k])
    greens = [jnp.where(k < used_blocks, greens[k], 0.0) for k in range(slots)]
    return jnp.stack(greens, 1)


def body(energies, h_blocks, couplings, shift_real, shift_rate, screened, sources, counts):
    used_blocks = counts[0]
    hams = h_blocks[0]
    links = couplings[0]
    batch = energies.shape[0]
    diag_a = build_blocks(energies, hams, shift_real[:, 0], shift_rate[:, 0])
    summary = summary_masked(diag_a, links, used_blocks)
    entry_link = jnp.broadcast_to(links[0], (batch,) + links[0].shape)
    own_item = summary + (entry_link, jnp.zeros((batch,), jnp.float32))
    zero_block = jnp.zeros_like(entry_link)
    identity_item = (
        zero_block,
        zero_block,
        zero_block,
        zero_block,
        zero_block,
        jnp.ones((batch,), jnp.float32),
    )
    before = carried_in(own_item, "seg", join_segments, identity_item, False)
    after = carried_in(own_item, "seg", join_reversed, identity_item, True)
    right_link = after[4]
    sig_right = complex_product(complex_product(right_link, after[0]), adjoint(right_link))
    greens = greens_masked(diag_a, links, used_blocks, before[3], sig_right)
    packed = greens.astype(jnp.bfloat16)
    weights = screened[:, 0][:, None]
    portion = lax.all_gather(packed, "energy", axis=0, tiled=True)
    energy_index = jnp.arange(portion.shape[0], dtype=jnp.int32)
    selector = (jnp.transpose(sources)[:, :, None] == energy_index[None, None, :]).astype(
        jnp.bfloat16
    )
    picked = jnp.einsum("jtc,cmab->jtmab", selector, portion, preferred_element_type=jnp.float32)
    sigma_local = jnp.sum(entry_product(picked, weights), 0)
    return sigma_local[:, None]


def solution(mesh):
    in_specs = (
        P("energy"),
        P("seg", None, None, None),
        P("seg", None, None, None),
        P("energy", "seg", None),
        P("energy", "seg", None),
        P(None, "seg", None, None, None),
        P("energy", None),
        P("seg"),
    )
    out_specs = P("energy", "seg", None, None, None)
    return jax.shard_map(body, mesh=mesh, in_specs=in_specs, out_specs=out_specs, check_vma=False)
```

profile of v0, /device:TPU:1, one launch (start us, length us, event | category | flops | bytes accessed | tf_op | source)
XLA Modules:
  0.0 914.6 jit_solution(2029570520931894767)
XLA Ops:
  13.0 11.7 %custom-call.42 = f32[1,128,128]{2,1,0:T(8,128)S(1)} custom-call(f32[1,128,128]{2,1,0:T(8,128)S(1)} %fusion.303), custom_call_target="Cholesky" | custom-call | tf_op jit(solution)/shard_map/jit(cholesky)/cholesky/custom-call.1 | solution.py:56
  38.2 11.7 %custom-call.45 = f32[1,128,128]{2,1,0:T(8,128)S(1)} custom-call(f32[1,128,128]{2,1,0:T(8,128)S(1)} %fusion.300), custom_call_target="Cholesky" | custom-call | tf_op jit(solution)/shard_map/jit(cholesky)/cholesky/custom-call.1 | solution.py:56
  64.3 11.7 %custom-call.48 = f32[1,128,128]{2,1,0:T(8,128)S(1)} custom-call(f32[1,128,128]{2,1,0:T(8,128)S(1)} %fusion.297), custom_call_target="Cholesky" | custom-call | tf_op jit(solution)/shard_map/jit(cholesky)/cholesky/custom-call.1 | solution.py:56
  91.7 34.4 %all-reduce.2 = f32[16]{0:T(128)S(1)} all-reduce(f32[16]{0:T(128)S(1)} %dynamic-update-slice), channel_id=1, replica_groups=mesh['energy'=32,'seg'=16] {'seg'}, use_global_device_ids=true, to_apply=%add.2 | all-reduce | flops 16 | bytes 128
  128.4 11.7 %custom-call.51 = f32[1,128,128]{2,1,0:T(8,128)S(1)} custom-call(f32[1,128,128]{2,1,0:T(8,128)S(1)} %fusion.294), custom_call_target="Cholesky" | custom-call | tf_op jit(solution)/shard_map/jit(cholesky)/cholesky/custom-call.1 | solution.py:56
  153.9 15.7 %all_gather.20 = f32[16,1,64,128]{3,2,1,0:T(8,128)S(1)} all-gather(f32[1,1,64,128]{3,2,1,0:T(8,128)S(1)} %copy.144), channel_id=1, replica_groups=mesh['energy'=32,'seg'=16] {'seg'}, dimensions={0}, use_global_device_ids=true | all-gather | bytes 557056 | tf_op jit(solution)/shard_map/all_gather | solution.py:13
  169.6 18.4 %all_gather.45 = f32[16,1,64,128]{3,2,1,0:T(8,128)S(1)} all-gather(f32[1,1,64,128]{3,2,1,0:T(8,128)S(1)} %get-tuple-element.496), channel_id=1, replica_groups=mesh['energy'=32,'seg'=16] {'seg'}, dimensions={0}, use_global_device_ids=true | all-gather | bytes 557056 | tf_op jit(solution)/shard_map/all_gather | solution.py:13
  187.9 16.6 %all-gather.2 = f32[1024,128]{1,0:T(8,128)S(1)} all-gather(f32[64,128]{1,0:T(8,128)S(1)} %copy.156), channel_id=4, replica_groups=mesh['energy'=32,'seg'=16] {'seg'}, dimensions={0}, use_global_device_ids=true | all-gather | bytes 557056 | tf_op jit(solution)/shard_map/all_gather | solution.py:13
  204.6 18.1 %all-gather.1 = f32[1024,128]{1,0:T(8,128)S(1)} all-gather(f32[64,128]{1,0:T(8,128)S(1)} %copy.154), channel_id=3, replica_groups=mesh['energy'=32,'seg'=16] {'seg'}, dimensions={0}, use_global_device_ids=true | all-gather | bytes 557056 | tf_op jit(solution)/shard_map/all_gather | solution.py:13
  222.7 17.2 %all-gather = f32[1024,128]{1,0:T(8,128)S(1)} all-gather(f32[64,128]{1,0:T(8,128)S(1)} %copy.148), channel_id=2, replica_groups=mesh['energy'=32,'seg'=16] {'seg'}, dimensions={0}, use_global_device_ids=true | all-gather | bytes 557056 | tf_op jit(solution)/shard_map/all_gather | solution.py:13
  239.9 441.0 %while.40 = (s32[]{:T(128)}, f32[1,64,128]{2,1,0:T(8,128)S(1)}, f32[1,64,128]{2,1,0:T(8,128)S(1)}, f32[1]{0:T(128)}, s32[]{:T(128)}, /*index=5*/f32[16,1]{0,1:T(...) while((s32[]{:T(128)}, f32[1,64,128]{2,1,0:T(8,128)S(1)}, ...), condition=%wide.region_5.9_spmd, body=%wide.region_4.8_spmd.sunk | while | flops 151679104 | bytes 3040514 | solution.py:22
  244.5 11.7 %custom-call.72 = f32[1,128,128]{2,1,0:T(8,128)S(1)} custom-call(f32[1,128,128]{2,1,0:T(8,128)S(1)} %fusion.536), custom_call_target="Cholesky" | custom-call | tf_op jit(solution)/shard_map/while/body/jit(cholesky)/cholesky/custom-call.1 | solution.py:56
  273.9 11.7 %custom-call.72 = f32[1,128,128]{2,1,0:T(8,128)S(1)} custom-call(f32[1,128,128]{2,1,0:T(8,128)S(1)} %fusion.536), custom_call_target="Cholesky" | custom-call | tf_op jit(solution)/shard_map/while/body/jit(cholesky)/cholesky/custom-call.1 | solution.py:56
  303.3 11.7 %custom-call.72 = f32[1,128,128]{2,1,0:T(8,128)S(1)} custom-call(f32[1,128,128]{2,1,0:T(8,128)S(1)} %fusion.536), custom_call_target="Cholesky" | custom-call | tf_op jit(solution)/shard_map/while/body/jit(cholesky)/cholesky/custom-call.1 | solution.py:56
  332.6 11.7 %custom-call.72 = f32[1,128,128]{2,1,0:T(8,128)S(1)} custom-call(f32[1,128,128]{2,1,0:T(8,128)S(1)} %fusion.536), custom_call_target="Cholesky" | custom-call | tf_op jit(solution)/shard_map/while/body/jit(cholesky)/cholesky/custom-call.1 | solution.py:56
  362.0 11.7 %custom-call.72 = f32[1,128,128]{2,1,0:T(8,128)S(1)} custom-call(f32[1,128,128]{2,1,0:T(8,128)S(1)} %fusion.536), custom_call_target="Cholesky" | custom-call | tf_op jit(solution)/shard_map/while/body/jit(cholesky)/cholesky/custom-call.1 | solution.py:56
  391.4 11.7 %custom-call.72 = f32[1,128,128]{2,1,0:T(8,128)S(1)} custom-call(f32[1,128,128]{2,1,0:T(8,128)S(1)} %fusion.536), custom_call_target="Cholesky" | custom-call | tf_op jit(solution)/shard_map/while/body/jit(cholesky)/cholesky/custom-call.1 | solution.py:56
  420.8 11.7 %custom-call.72 = f32[1,128,128]{2,1,0:T(8,128)S(1)} custom-call(f32[1,128,128]{2,1,0:T(8,128)S(1)} %fusion.536), custom_call_target="Cholesky" | custom-call | tf_op jit(solution)/shard_map/while/body/jit(cholesky)/cholesky/custom-call.1 | solution.py:56
  450.2 11.7 %custom-call.72 = f32[1,128,128]{2,1,0:T(8,128)S(1)} custom-call(f32[1,128,128]{2,1,0:T(8,128)S(1)} %fusion.536), custom_call_target="Cholesky" | custom-call | tf_op jit(solution)/shard_map/while/body/jit(cholesky)/cholesky/custom-call.1 | solution.py:56
  479.6 11.7 %custom-call.72 = f32[1,128,128]{2,1,0:T(8,128)S(1)} custom-call(f32[1,128,128]{2,1,0:T(8,128)S(1)} %fusion.536), custom_call_target="Cholesky" | custom-call | tf_op jit(solution)/shard_map/while/body/jit(cholesky)/cholesky/custom-call.1 | solution.py:56
  508.9 11.7 %custom-call.72 = f32[1,128,128]{2,1,0:T(8,128)S(1)} custom-call(f32[1,128,128]{2,1,0:T(8,128)S(1)} %fusion.536), custom_call_target="Cholesky" | custom-call | tf_op jit(solution)/shard_map/while/body/jit(cholesky)/cholesky/custom-call.1 | solution.py:56
  538.3 11.7 %custom-call.72 = f32[1,128,128]{2,1,0:T(8,128)S(1)} custom-call(f32[1,128,128]{2,1,0:T(8,128)S(1)} %fusion.536), custom_call_target="Cholesky" | custom-call | tf_op jit(solution)/shard_map/while/body/jit(cholesky)/cholesky/custom-call.1 | solution.py:56
  771.3 11.9 %custom-call.63 = f32[1,128,128]{2,1,0:T(8,128)S(1)} custom-call(f32[1,128,128]{2,1,0:T(8,128)S(1)} %fusion.282), custom_call_target="Cholesky" | custom-call | tf_op jit(solution)/shard_map/jit(cholesky)/cholesky/custom-call.1 | solution.py:56
  798.4 103.4 %all-gather.5.cloned.1.call-done = bf16[32,4,64,128]{3,2,1,0:T(8,128)(2,1)} async-done(((bf16[1,4,64,128]{3,2,1,0:T(8,128)(2,1)}), bf16[32,4,64,128]{3,2,1,0:T(8,128)(2,1)}) %all-gather.5.cloned.1.call-update) | async-done | bytes 2097168 | tf_op jit(solution)/shard_map/all_gather | solution.py:208
  (703 shorter events, 474.3 us)
Async XLA Ops:
  6.5 895.2 %all-gather.5.cloned.1.call-start = ((), (), s32[]{:S(2)}) async-start(), calls=%async_computation | async-start | bytes 2162688 | tf_op jit(solution)/shard_map/all_gather | solution.py:208
  12.4 25.3 %copy-start.9 = (f32[64,128]{0,1:T(8,128)}, f32[64,128]{0,1:T(8,128)S(1)}, u32[]{:S(2)}) copy-start(f32[64,128]{0,1:T(8,128)S(1)} %get-tuple-element.495) | copy-start | bytes 98308
  12.9 113.6 %copy-start.19 = (f32[64,128]{1,0:T(8,128)}, f32[64,128]{1,0:T(8,128)S(1)}, u32[]{:S(2)}) copy-start(f32[64,128]{1,0:T(8,128)S(1)} %get-tuple-element.497) | copy-start | bytes 98308
  36.6 25.3 %copy-start.5 = (f32[64,64]{1,0:T(8,128)}, f32[64,64]{1,0:T(8,128)S(1)}, u32[]{:S(2)}) copy-start(f32[64,64]{1,0:T(8,128)S(1)} %get-tuple-element.607) | copy-start | bytes 49156
  36.6 25.3 %copy-start.7 = (f32[64,64]{1,0:T(8,128)}, f32[64,64]{1,0:T(8,128)S(1)}, u32[]{:S(2)}) copy-start(f32[64,64]{1,0:T(8,128)S(1)} %get-tuple-element.610) | copy-start | bytes 49156
  36.6 89.9 %copy-start.11 = (f32[64,64]{0,1:T(8,128)}, f32[64,64]{0,1:T(8,128)S(1)}, u32[]{:S(2)}) copy-start(f32[64,64]{0,1:T(8,128)S(1)} %get-tuple-element.614) | copy-start | bytes 49156
  36.6 89.9 %copy-start.13 = (f32[64,64]{0,1:T(8,128)}, f32[64,64]{0,1:T(8,128)S(1)}, u32[]{:S(2)}) copy-start(f32[64,64]{0,1:T(8,128)S(1)} %get-tuple-element.615) | copy-start | bytes 49156
  88.5 63.3 %copy-start.1 = (f32[64,64]{1,0:T(8,128)}, f32[64,64]{1,0:T(8,128)S(1)}, u32[]{:S(2)}) copy-start(f32[64,64]{1,0:T(8,128)S(1)} %get-tuple-element.599) | copy-start | bytes 49156
  88.5 63.3 %copy-start.3 = (f32[64,64]{1,0:T(8,128)}, f32[64,64]{1,0:T(8,128)S(1)}, u32[]{:S(2)}) copy-start(f32[64,64]{1,0:T(8,128)S(1)} %get-tuple-element.602) | copy-start | bytes 49156
  88.5 63.3 %copy-start.15 = (f32[64,64]{0,1:T(8,128)}, f32[64,64]{0,1:T(8,128)S(1)}, u32[]{:S(2)}) copy-start(f32[64,64]{0,1:T(8,128)S(1)} %get-tuple-element.600) | copy-start | bytes 49156
  88.5 63.4 %copy-start.17 = (f32[64,64]{0,1:T(8,128)}, f32[64,64]{0,1:T(8,128)S(1)}, u32[]{:S(2)}) copy-start(f32[64,64]{0,1:T(8,128)S(1)} %get-tuple-element.601) | copy-start | bytes 49156
  691.2 28.0 %copy-start.6 = (f32[64,64]{1,0:T(8,128)S(1)}, f32[64,64]{1,0:T(8,128)}, u32[]{:S(2)}) copy-start(f32[64,64]{1,0:T(8,128)} %copy-done.5) | copy-start | bytes 49156
  691.2 28.0 %copy-start.8 = (f32[64,64]{1,0:T(8,128)S(1)}, f32[64,64]{1,0:T(8,128)}, u32[]{:S(2)}) copy-start(f32[64,64]{1,0:T(8,128)} %copy-done.7) | copy-start | bytes 49156
  691.2 28.3 %copy-start.21 = (f32[64,64]{0,1:T(8,128)S(1)}, f32[64,64]{0,1:T(8,128)}, u32[]{:S(2)}) copy-start(f32[64,64]{0,1:T(8,128)} %copy-done.20) | copy-start | bytes 49156
  691.3 28.3 %copy-start.23 = (f32[64,64]{0,1:T(8,128)S(1)}, f32[64,64]{0,1:T(8,128)}, u32[]{:S(2)}) copy-start(f32[64,64]{0,1:T(8,128)} %copy-done.22) | copy-start | bytes 49156
  691.3 28.6 %copy-start.10 = (f32[64,128]{0,1:T(8,128)S(1)}, f32[64,128]{0,1:T(8,128)}, u32[]{:S(2)}) copy-start(f32[64,128]{0,1:T(8,128)} %copy-done.9) | copy-start | bytes 98308
  695.0 49.8 %copy-start.12 = (f32[64,64]{0,1:T(8,128)S(1)}, f32[64,64]{0,1:T(8,128)}, u32[]{:S(2)}) copy-start(f32[64,64]{0,1:T(8,128)} %copy-done.11) | copy-start | bytes 49156
  695.0 49.8 %copy-start.14 = (f32[64,64]{0,1:T(8,128)S(1)}, f32[64,64]{0,1:T(8,128)}, u32[]{:S(2)}) copy-start(f32[64,64]{0,1:T(8,128)} %copy-done.13) | copy-start | bytes 49156
  720.2 49.3 %copy-start.2 = (f32[64,64]{1,0:T(8,128)S(1)}, f32[64,64]{1,0:T(8,128)}, u32[]{:S(2)}) copy-start(f32[64,64]{1,0:T(8,128)} %copy-done.1) | copy-start | bytes 49156
  720.2 49.3 %copy-start.4 = (f32[64,64]{1,0:T(8,128)S(1)}, f32[64,64]{1,0:T(8,128)}, u32[]{:S(2)}) copy-start(f32[64,64]{1,0:T(8,128)} %copy-done.3) | copy-start | bytes 49156
  720.3 49.6 %copy-start.16 = (f32[64,64]{0,1:T(8,128)S(1)}, f32[64,64]{0,1:T(8,128)}, u32[]{:S(2)}) copy-start(f32[64,64]{0,1:T(8,128)} %copy-done.15) | copy-start | bytes 49156
  720.3 49.6 %copy-start.18 = (f32[64,64]{0,1:T(8,128)S(1)}, f32[64,64]{0,1:T(8,128)}, u32[]{:S(2)}) copy-start(f32[64,64]{0,1:T(8,128)} %copy-done.17) | copy-start | bytes 49156
  770.5 27.4 %copy-start = (f32[8,1,4,64,128]{4,3,2,1,0:T(8,128)S(1)}, f32[8,1,4,64,128]{4,3,2,1,0:T(8,128)}, u32[]{:S(2)}) copy-start(f32[8,1,4,64,128]{4,3,2,1,0:T(8,128)} %param.22) | copy-start | bytes 3145732
  798.0 103.8 %copy-start.25 = (s32[1,8]{1,0:T(1,128)S(1)}, s32[1,8]{1,0:T(1,128)}, u32[]{:S(2)}) copy-start(s32[1,8]{1,0:T(1,128)} %param.23) | copy-start | bytes 100
  (3 other events, 31.6 us)
Sparse Core Ops, SparseCore 0:
  798.1 103.6 all-gather.4
where the time goes:
time: 924 us; the launch traced here: 915 us
  other arithmetic  565 us (61%)
  blocking collectives  120 us (13%)
  waiting for transfers between devices  103 us (11%)
  matrix products  78.3 us (8%)
  loops' own time  21.3 us (2%)
  between operations  16.6 us (2%)
  local copies, waits for them, and re-layouts  9.55 us (1%)
    another operation x69, other arithmetic, complex_inverse(): factor = jnp.linalg.cholesky(normal)  286 us
    another operation x46, other arithmetic, complex_inverse(): jax.scipy.linalg.solve_triangular(factor, middle, lower=True, trans=1)  241 us
    all_gather x1, waiting for transfers between devices, body(): portion = lax.all_gather(packed, 'energy', axis=0, tiled=True)  103 us
    all_gather x5, blocking collectives, carried_in(): gathered = jax.tree.map(lambda a: lax.all_gather(a, axis), part)  86 us
    dot_general x159, matrix products, complex_product(): return jnp.matmul(matrix, expand(other), precision=lax.Precision.HIGHEST)  56.9 us
    unnamed x1, blocking collectives  34.4 us
    another operation x2, loops' own time, carried_in(): return lax.fori_loop(0, ahead, one, state)  21.3 us
  transfers between devices with their start and end apart: 1, of which 1 were waited for; matrix products, arithmetic and copies ran while one was open for 0% of the time, Pallas kernels for 0%

commit v1 on v0

v1 whole, which is shorter than its diff:
```python
import functools

import jax
import jax.numpy as jnp
from jax import lax
from jax.experimental import pallas as pl
from jax.experimental.pallas import tpu as pltpu
from jax.sharding import PartitionSpec as P

BS = 64
SLOTS = 4
WIDE = 2 * BS
broadening = 0.02
f32 = jnp.float32
bf16 = jnp.bfloat16
MESH = pl.DeviceIdType.MESH


def times_i(m):
    lane = lax.broadcasted_iota(jnp.int32, m.shape, 1)
    turned = pltpu.roll(m, BS, 1)
    return jnp.where(lane < BS, -turned, turned)


def expand(m):
    return jnp.concatenate([m, times_i(m)], 0)


def products(lefts, rights):
    left = lefts[0] if len(lefts) == 1 else jnp.concatenate(lefts, 0)
    right = [expand(m) for m in rights]
    right = right[0] if len(right) == 1 else jnp.concatenate(right, 1)
    out = jnp.dot(left, right, precision=lax.Precision.HIGHEST, preferred_element_type=f32)
    return [
        [out[BS * i : BS * i + BS, WIDE * j : WIDE * j + WIDE] for j in range(len(rights))]
        for i in range(len(lefts))
    ]


def product(a, b):
    return products([a], [b])[0][0]


def adjoint(m):
    t = jnp.transpose(m)
    return jnp.concatenate([t[:BS], -t[BS:]], 1)


def inverses(mats):
    lane8 = lax.broadcasted_iota(jnp.int32, (8, WIDE), 1)
    row8 = lax.broadcasted_iota(jnp.int32, (8, WIDE), 0)
    lane = lax.broadcasted_iota(jnp.int32, (BS, WIDE), 1)
    mats = list(mats)
    for p in range(BS // 8):
        own = (lane8 & (BS - 1)) // 8 == p
        panel = (lane & (BS - 1)) // 8 == p
        for b, m in enumerate(mats):
            rows = m[8 * p : 8 * p + 8]
            col_re = [jnp.broadcast_to(m[:, 8 * p + k : 8 * p + k + 1], (BS, WIDE)) for k in range(8)]
            col_im = [
                jnp.broadcast_to(m[:, BS + 8 * p + k : BS + 8 * p + k + 1], (BS, WIDE)) for k in range(8)
            ]
            x = jnp.where(own, jnp.where(lane8 == row8 + 8 * p, 1.0, 0.0), rows)
            z = jnp.where(own, jnp.where(lane8 == row8 + (8 * p + BS), 1.0, 0.0), times_i(rows))
            c_re = [c[8 * p : 8 * p + 8] for c in col_re]
            c_im = [c[8 * p : 8 * p + 8] for c in col_im]
            for k in range(8):
                p_re = jnp.broadcast_to(c_re[k][k : k + 1], (8, WIDE))
                p_im = jnp.broadcast_to(c_im[k][k : k + 1], (8, WIDE))
                scale = 1.0 / (p_re * p_re + p_im * p_im)
                q_re, q_im = p_re * scale, -(p_im * scale)
                x_k = jnp.broadcast_to(x[k : k + 1], (8, WIDE))
                z_k = jnp.broadcast_to(z[k : k + 1], (8, WIDE))
                x_s, z_s = x_k * q_re + z_k * q_im, z_k * q_re - x_k * q_im
                m_re, m_im = c_re[k], c_im[k]
                pivot = row8 == k
                for j in range(k + 1, 8):
                    r_re = jnp.broadcast_to(c_re[j][k : k + 1], (8, WIDE))
                    r_im = jnp.broadcast_to(c_im[j][k : k + 1], (8, WIDE))
                    s_re, s_im = r_re * q_re - r_im * q_im, r_re * q_im + r_im * q_re
                    c_re[j] = jnp.where(pivot, s_re, c_re[j] - (m_re * s_re - m_im * s_im))
                    c_im[j] = jnp.where(pivot, s_im, c_im[j] - (m_re * s_im + m_im * s_re))
                x, z = (
                    jnp.where(pivot, x_s, x - (m_re * x_s + m_im * z_s)),
                    jnp.where(pivot, z_s, z - (m_re * z_s - m_im * x_s)),
                )
            total = None
            for k in range(8):
                term = col_re[k] * x[k : k + 1] + col_im[k] * z[k : k + 1]
                total = term if total is None else total + term
            rest = jnp.where(panel, 0.0, m) - total
            parts = [x if q == p else rest[8 * q : 8 * q + 8] for q in range(BS // 8)]
            mats[b] = jnp.concatenate(parts, 0)
    return mats


def kernel(
    n_energy, n_seg,
    counts, sources, energies, h_ref, u_ref, real_ref, rate_ref, screened_hbm,
    out_ref,
    a_all, w_all, v_all, keep, factors, state, outbox, from_left, from_right, half_in,
    g_out, g_in, gathered, screened, turned,
    load_sem, left_send, left_recv, right_send, right_recv, half_send, half_recv,
    g_send, g_recv, ring_send, ring_recv, pair_send, pair_recv,
):
    e = lax.axis_index("energy")
    s = lax.axis_index("seg")
    n_z = n_energy // 2
    core = e % 2
    up_e = (e + 2) % n_energy
    down_e = (e + n_energy - 2) % n_energy
    pair_e = e + 1 - 2 * core

    barrier = pltpu.get_barrier_semaphore()
    hops = []
    h = 1
    while h < n_seg:
        hops.append(h)
        h *= 2
    greeted = [(up_e, s), (down_e, s), (pair_e, s)]
    for h in hops[:-1]:
        greeted += [(e, (s + h) % n_seg), (e, (s + n_seg - h) % n_seg)]
    greeted.append((e, (s + n_seg // 2) % n_seg))
    for device in greeted:
        pl.semaphore_signal(barrier, inc=1, device_id=device, device_id_type=MESH)

    load = pltpu.make_async_copy(screened_hbm, screened, load_sem)
    load.start()

    count = counts[0]
    energy = energies[0]
    row = lax.broadcasted_iota(jnp.int32, (BS, WIDE), 0)
    lane = lax.broadcasted_iota(jnp.int32, (BS, WIDE), 1)
    diagonal = (lane & (BS - 1)) == row
    attached = jnp.where(s > 0, 1.0, 0.0).astype(f32)
    for k in range(SLOTS):
        real = energy - real_ref[0, :, BS * k : BS * k + BS]
        imag = broadening + rate_ref[0, :, BS * k : BS * k + BS]
        line = jnp.concatenate([real, imag], 1)
        a_all[k] = jnp.where(diagonal, line, 0.0) - h_ref[0, k]
        w = u_ref[0, k]
        if k == 0:
            w = w * attached
        w_all[k] = w
        v_all[k] = adjoint(w)

    slot = [jnp.maximum(count + (place - SLOTS), 0) for place in range(SLOTS)]
    a = [a_all[i] for i in slot]
    w = [w_all[i] for i in slot]
    v = [v_all[i] for i in slot]
    many = jnp.full((BS, WIDE), count, jnp.int32)
    has0, has1, has2 = many >= 4, many >= 3, many >= 2

    g0, g2 = inverses([a[0], a[2]])
    ((g0w1, g0v0),) = products([g0], [w[1], v[0]])
    ((g2w3, g2v2),) = products([g2], [w[3], v[2]])
    (u01, d0l), (d01, l10) = products([w[0], v[1]], [g0w1, g0v0])
    (u23, d2x), (d2r, l32) = products([w[2], v[3]], [g2w3, g2v2])
    d1 = a[1] - jnp.where(has0, d01, 0.0) - d2x
    ul1 = jnp.where(has0, u01, w[1])
    l1l = jnp.where(has0, l10, v[1])
    (g1,) = inverses([d1])
    ((b1r, b1l),) = products([g1], [u23, l1l])
    (u13, d1l), (d1r, l31) = products([ul1, l32], [b1r, b1l])
    u_own = jnp.where(has1, u13, jnp.where(has2, u23, w[3]))
    l_own = jnp.where(has1, l31, jnp.where(has2, l32, v[3]))
    sigma_left = jnp.where(has1, d1r, 0.0) + jnp.where(has2, d2r, 0.0)
    to_left = jnp.where(has0, d0l, 0.0) + jnp.where(has1, d1l, jnp.where(has2, d2x, 0.0))

    outbox[0, 1] = u_own
    outbox[0, 2] = l_own
    outbox[0, 3] = to_left
    keep[0] = a[3]
    keep[1] = u_own
    keep[2] = l_own
    pl.semaphore_wait(barrier, len(greeted))

    def right_copy(level, h):
        return pltpu.make_async_remote_copy(
            src_ref=outbox.at[level, pl.ds(0, 3)],
            dst_ref=from_left.at[level],
            send_sem=right_send.at[level],
            recv_sem=left_recv.at[level],
            device_id=(e, (s + h) % n_seg),
            device_id_type=MESH,
        )

    def left_copy(level, h):
        return pltpu.make_async_remote_copy(
            src_ref=outbox.at[level, pl.ds(1, 3)],
            dst_ref=from_right.at[level],
            send_sem=left_send.at[level],
            recv_sem=right_recv.at[level],
            device_id=(e, (s + n_seg - h) % n_seg),
            device_id_type=MESH,
        )

    def start_left(level, h):
        @pl.when(s >= h)
        def _():
            left_copy(level, h).start()

    def start_right(level, h):
        @pl.when(s + h < n_seg)
        def _():
            right_copy(level, h).start()

    def await_right(level, h):
        @pl.when(s + h < n_seg)
        def _():
            left_copy(level, h).wait_recv()

    def await_left(level, h):
        @pl.when(s >= h)
        def _():
            right_copy(level, h).wait_recv()

    start_left(0, 1)
    here = jnp.full((BS, WIDE), s, jnp.int32)

    def interior_factors():
        ((cl1,), (cr1,)) = products([ul1, l32], [g1])
        ((w0g0,), (v1g0,)) = products([w[0], v[1]], [g0])
        ((w2g2,), (v3g2,)) = products([w[2], v[3]], [g2])
        ((p0l, p0r, p0g), (p2l, p2r, p2g)) = products([g0w1, g2v2], [b1l, b1r, g1])
        ((q0l,), (q0r,), (i0,)) = products([cl1, cr1, p0g], [v1g0])
        ((q2l,), (q2r,), (i2,)) = products([cl1, cr1, p2g], [w2g2])
        factors[0, 0], factors[1, 0], factors[2, 0] = g0v0 + p0l, b1l, jnp.where(has1, p2l, g2v2)
        factors[0, 1], factors[1, 1], factors[2, 1] = p0r, b1r, g2w3 + jnp.where(has1, p2r, 0.0)
        factors[0, 2], factors[1, 2], factors[2, 2] = w0g0 + q0l, cl1, jnp.where(has1, q2l, w2g2)
        factors[0, 3], factors[1, 3], factors[2, 3] = q0r, cr1, v3g2 + jnp.where(has1, q2r, 0.0)
        factors[0, 4], factors[1, 4], factors[2, 4] = g0 + i0, g1, g2 + jnp.where(has1, i2, 0.0)

    interior_factors()

    state[0] = sigma_left
    state[1] = u_own
    state[2] = l_own
    await_right(0, 1)
    joined = here + 1 < n_seg
    first_right = jnp.where(joined, from_right[0, 2], 0.0)
    keep[3] = first_right
    state[3] = jnp.where(joined, from_right[0, 0], 0.0)
    state[4] = jnp.where(joined, from_right[0, 1], 0.0)
    state[5] = first_right

    for level, h in enumerate(hops[:-1], 1):
        (inner,) = inverses([keep[0] - state[0] - state[5]])
        ((to_r, to_l),) = products([inner], [state[3], state[2]])
        ((add_r, l_new), (u_new, add_l)) = products([state[4], state[1]], [to_r, to_l])
        outbox[level, 0] = add_r
        outbox[level, 1] = u_new
        outbox[level, 2] = l_new
        outbox[level, 3] = add_l
        start_right(level, h)
        start_left(level, h)
        if level == 1:
            load.wait()
            for j in range(screened.shape[0]):
                for k in range(SLOTS):
                    turned[j, k] = pltpu.roll(screened[j, 0, k], BS, 1)
        await_left(level, h)
        joined = here >= h
        state[0] = state[0] + jnp.where(joined, from_left[level, 0], 0.0)
        state[1] = jnp.where(joined, from_left[level, 1], 0.0)
        state[2] = jnp.where(joined, from_left[level, 2], 0.0)
        await_right(level, h)
        joined = here + h < n_seg
        state[3] = jnp.where(joined, from_right[level, 0], 0.0)
        state[4] = jnp.where(joined, from_right[level, 1], 0.0)
        state[5] = state[5] + jnp.where(joined, from_right[level, 2], 0.0)

    lower = here < n_seg // 2
    (inner,) = inverses([keep[0] - state[0] - state[5]])
    near = product(inner, jnp.where(lower, state[3], state[2]))
    half_in[0] = product(jnp.where(lower, state[4], state[1]), near)
    half = pltpu.make_async_remote_copy(
        src_ref=half_in.at[0],
        dst_ref=half_in.at[1],
        send_sem=half_send,
        recv_sem=half_recv,
        device_id=(e, (s + n_seg // 2) % n_seg),
        device_id_type=MESH,
    )
    half.start()
    half.wait_recv()
    arrived = half_in[1]
    sigma_left = state[0] + jnp.where(lower, 0.0, arrived)
    sigma_right = state[5] + jnp.where(lower, arrived, 0.0)

    g_rep, g_end = inverses(
        [keep[0] - sigma_left - sigma_right, keep[0] - sigma_left - keep[3]]
    )
    g_out[...] = g_end
    end_copy = pltpu.make_async_remote_copy(
        src_ref=g_out,
        dst_ref=g_in,
        send_sem=g_send,
        recv_sem=g_recv,
        device_id=(e, (s + 1) % n_seg),
        device_id_type=MESH,
    )

    @pl.when(s + 1 < n_seg)
    def _():
        end_copy.start()

    far = n_z // 2
    pieces = [(SLOTS - 1, 1), (0, SLOTS - 1)]
    split = [(0, 2), (2, 2)]

    def ring_copy(way, d, piece):
        first, size = pieces[piece] if d < far else split[way]
        if way == 0:
            owner, target = (e + 2 * (n_energy - d + 1)) % n_energy, up_e
        else:
            owner, target = (e + 2 * (d - 1)) % n_energy, down_e
        block = gathered.at[owner, pl.ds(first, size)]
        return pltpu.make_async_remote_copy(
            src_ref=block,
            dst_ref=block,
            send_sem=ring_send.at[way, d - 1, piece],
            recv_sem=ring_recv.at[way, d - 1, piece],
            device_id=(target, s),
            device_id_type=MESH,
        )

    def ring_arrival(way, d, piece):
        first, size = pieces[piece] if d < far else split[way]
        owner = (e + 2 * (n_energy - d)) % n_energy if way == 0 else (e + 2 * d) % n_energy
        block = gathered.at[owner, pl.ds(first, size)]
        pltpu.make_async_remote_copy(
            src_ref=block,
            dst_ref=block,
            send_sem=ring_send.at[way, d - 1, piece],
            recv_sem=ring_recv.at[way, d - 1, piece],
            device_id=(up_e if way == 0 else down_e, s),
            device_id_type=MESH,
        ).wait_recv()

    def pair_copy(way, d, piece, arriving=False):
        first, size = pieces[piece] if d < far else split[way]
        base = pair_e if arriving else e
        owner = (base + 2 * (n_energy - d)) % n_energy if way == 0 else (base + 2 * d) % n_energy
        block = gathered.at[owner, pl.ds(first, size)]
        return pltpu.make_async_remote_copy(
            src_ref=block,
            dst_ref=block,
            send_sem=pair_send.at[way, d, piece],
            recv_sem=pair_recv.at[way, d, piece],
            device_id=(pair_e, s),
            device_id_type=MESH,
        )

    def start_own(piece):
        for way in range(2):
            if far > 1:
                ring_copy(way, 1, piece).start()
        pair_copy(0, 0, piece).start()

    gathered[e, SLOTS - 1] = g_rep.astype(bf16)
    start_own(0)

    @pl.when(s > 0)
    def _():
        end_copy.wait_recv()

    g_left = jnp.where(here > 0, g_in[...], 0.0)
    bl = [factors[m, 0] for m in range(3)]
    cl = [factors[m, 2] for m in range(3)]
    k1 = [r[0] for r in products(bl, [g_left])]
    k2 = products([g_left], cl)[0]
    t1 = [r[0] for r in products(k1, [keep[1]])]
    t2 = products([keep[2]], k2)[0]
    direct = [product(k1[m], cl[m]) for m in range(3)]
    t3 = [r[0] for r in products([t1[m] + factors[m, 1] for m in range(3)], [g_rep])]
    for m in range(3):
        g_m = factors[m, 4] + direct[m] + product(t3[m], t2[m] + factors[m, 3])
        gathered[e, m] = g_m.astype(bf16)
    start_own(1)
    if far == 1:
        for way in range(2):
            ring_copy(way, 1, 0).start()

    for d in range(1, far):
        for piece in range(2):
            for way in range(2):
                ring_arrival(way, d, piece)
                if d + 1 < far:
                    ring_copy(way, d + 1, piece).start()
                elif piece == 1:
                    ring_copy(way, far, 0).start()
                pair_copy(way, d, piece).start()
    for way in range(2):
        ring_arrival(way, far, 0)
        pair_copy(way, far, 0).start()

    moved = [(0, 0, 0), (0, 0, 1)]
    for d in range(1, far):
        for way in range(2):
            for piece in range(2):
                ring_copy(way, d, piece).wait_send()
                moved.append((way, d, piece))
    for way in range(2):
        ring_copy(way, far, 0).wait_send()
        moved.append((way, far, 0))
    for way, d, piece in moved:
        pair_copy(way, d, piece).wait_send()
        pair_copy(way, d, piece, arriving=True).wait_recv()

    for level, h in enumerate([1] + hops[:-1]):

        @pl.when(s >= h)
        def _(level=level, h=h):
            left_copy(level, h).wait_send()

        if level > 0:

            @pl.when(s + h < n_seg)
            def _(level=level, h=h):
                right_copy(level, h).wait_send()

    half.wait_send()

    @pl.when(s + 1 < n_seg)
    def _():
        end_copy.wait_send()

    shifts = screened.shape[0]
    source = [sources[0, j] for j in range(shifts)]
    for k in range(SLOTS):
        place = jnp.minimum(SLOTS - count + k, SLOTS - 1)
        same = cross = None
        for j in range(shifts):
            g = gathered[source[j], place].astype(f32)
            one, other = g * screened[j, 0, k], g * turned[j, k]
            same = one if same is None else same + one
            cross = other if cross is None else cross + other
        value = jnp.where(lane < BS, same - pltpu.roll(same, BS, 1), cross + pltpu.roll(cross, BS, 1))
        out_ref[0, 0, k] = jnp.where(many > k, value, 0.0)


def body(n_energy, n_seg, energies, h_blocks, couplings, shift_real, shift_rate, screened, sources, counts):
    shifts = screened.shape[0]
    n_z = n_energy // 2
    far = n_z // 2
    levels = max(n_seg.bit_length() - 1, 1)
    vmem = pl.BlockSpec(memory_space=pltpu.VMEM)
    smem = pl.BlockSpec(memory_space=pltpu.SMEM)
    block = (BS, WIDE)
    dma = pltpu.SemaphoreType.DMA
    return pl.pallas_call(
        functools.partial(kernel, n_energy, n_seg),
        out_shape=jax.ShapeDtypeStruct((1, 1, SLOTS) + block, f32),
        in_specs=[smem, smem, smem, vmem, vmem, vmem, vmem, pl.BlockSpec(memory_space=pl.ANY)],
        out_specs=vmem,
        scratch_shapes=[
            pltpu.VMEM((SLOTS,) + block, f32),
            pltpu.VMEM((SLOTS,) + block, f32),
            pltpu.VMEM((SLOTS,) + block, f32),
            pltpu.VMEM((4,) + block, f32),
            pltpu.VMEM((3, 5) + block, f32),
            pltpu.VMEM((6,) + block, f32),
            pltpu.VMEM((levels, 4) + block, f32),
            pltpu.VMEM((levels, 3) + block, f32),
            pltpu.VMEM((levels, 3) + block, f32),
            pltpu.VMEM((2,) + block, f32),
            pltpu.VMEM(block, f32),
            pltpu.VMEM(block, f32),
            pltpu.VMEM((n_energy, SLOTS) + block, bf16),
            pltpu.VMEM((shifts, 1, SLOTS) + block, f32),
            pltpu.VMEM((shifts, SLOTS) + block, f32),
            dma,
            dma((levels,)),
            dma((levels,)),
            dma((levels,)),
            dma((levels,)),
            dma,
            dma,
            dma,
            dma,
            dma((2, far, 2)),
            dma((2, far, 2)),
            dma((2, far + 1, 2)),
            dma((2, far + 1, 2)),
        ],
        compiler_params=pltpu.CompilerParams(collective_id=0, has_side_effects=True),
        name="greens",
    )(counts, sources, energies, h_blocks, couplings, shift_real, shift_rate, screened)


def solution(mesh):
    in_specs = (
        P("energy"),
        P("seg", None, None, None),
        P("seg", None, None, None),
        P("energy", "seg", None),
        P("energy", "seg", None),
        P(None, "seg", None, None, None),
        P("energy", None),
        P("seg"),
    )
    out_specs = P("energy", "seg", None, None, None)
    run = functools.partial(body, mesh.shape["energy"], mesh.shape["seg"])
    return jax.shard_map(run, mesh=mesh, in_specs=in_specs, out_specs=out_specs, check_vma=False)
```

time: 924 us -> 98 us (0.11)
  the two profiles are of different devices: /device:TPU:1 before, /device:TPU:9 now
where the time goes in v1:
time: 98 us; the launch traced here: 97.8 us
  Pallas kernels  94.9 us (97%)
  local copies, waits for them, and re-layouts  1.57 us (2%)
  between operations  1.31 us (1%)
    pallas_call x1, Pallas kernels, body(): pl.pallas_call(functools.partial(kernel, n_energy, n_seg), out_shape=jax....  94.9 us

profile of v1, /device:TPU:9, one launch (start us, length us, event | category | flops | bytes accessed | tf_op | source)
XLA Modules:
  0.0 97.8 jit_solution(16449200683656664480)
XLA Ops:
  1.3 94.9 %greens.1 = f32[1,1,4,64,128]{4,3,2,1,0:T(8,128)} custom-call(s32[1]{0:T(128)S(6)} %copy.11.counts, s32[1,8]{1,0:T(1,128)} %sources.1, f32[1]{0:T(128)S(6)} %copy.10.energies, f32[1,4,64,128]{3,2,1,0:T(8,128)} %h_ref.1, f32[1,4,64,128]{3,2,1,0:T(8,128)} %u_ref.1, f32[1,1,256]{2,1,0:T(1,128)} %real_ref.1, f32[1,1,256]{2,1,0:T(1,128)} %rate_ref.1, ...), custom_call_target="tpu_custom_call" | custom-call | tf_op jit(solution)/shard_map/greens/pallas_call | solution.py:452
  96.2 1.6 %copy.12 = f32[1,1,4,64,128]{4,3,2,1,0:T(8,128)} copy(f32[1,1,4,64,128]{4,3,2,1,0:T(8,128)} %greens.1) | data formatting | bytes 262144

commit v2 on v1

--- a/solution.py
+++ b/solution.py
@@ -37,6 +37,10 @@
     ]
 
 
+def multiply(a, wide):
+    return jnp.dot(a, wide, precision=lax.Precision.HIGHEST, preferred_element_type=f32)
+
+
 def product(a, b):
     return products([a], [b])[0][0]
 
@@ -46,50 +50,70 @@
     return jnp.concatenate([t[:BS], -t[BS:]], 1)
 
 
-def inverses(mats):
+def inverses(mats, size=BS):
     lane8 = lax.broadcasted_iota(jnp.int32, (8, WIDE), 1)
     row8 = lax.broadcasted_iota(jnp.int32, (8, WIDE), 0)
     lane = lax.broadcasted_iota(jnp.int32, (BS, WIDE), 1)
     mats = list(mats)
-    for p in range(BS // 8):
-        own = (lane8 & (BS - 1)) // 8 == p
-        panel = (lane & (BS - 1)) // 8 == p
+    for start in range(0, BS, size):
+        group = (lane & (BS - 1)) // size == start // size
+        blocks = range(start // 8, (start + size) // 8)
+        held = [{q: m[8 * q : 8 * q + 8] for q in blocks} for m in mats]
+        for p in blocks:
+            own = (lane8 & (BS - 1)) // 8 == p
+            for rows in held:
+                mine = rows[p]
+                x = jnp.where(own, jnp.where(lane8 == row8 + 8 * p, 1.0, 0.0), mine)
+                z = jnp.where(own, jnp.where(lane8 == row8 + (8 * p + BS), 1.0, 0.0), times_i(mine))
+                c_re = [jnp.broadcast_to(mine[:, 8 * p + k : 8 * p + k + 1], (8, WIDE)) for k in range(8)]
+                c_im = [
+                    jnp.broadcast_to(mine[:, BS + 8 * p + k : BS + 8 * p + k + 1], (8, WIDE))
+                    for k in range(8)
+                ]
+                for k in range(8):
+                    p_re = jnp.broadcast_to(c_re[k][k : k + 1], (8, WIDE))
+                    p_im = jnp.broadcast_to(c_im[k][k : k + 1], (8, WIDE))
+                    scale = 1.0 / (p_re * p_re + p_im * p_im)
+                    q_re, q_im = p_re * scale, -(p_im * scale)
+                    x_k = jnp.broadcast_to(x[k : k + 1], (8, WIDE))
+                    z_k = jnp.broadcast_to(z[k : k + 1], (8, WIDE))
+                    x_s, z_s = x_k * q_re + z_k * q_im, z_k * q_re - x_k * q_im
+                    m_re, m_im = c_re[k], c_im[k]
+                    pivot = row8 == k
+                    for j in range(k + 1, 8):
+                        r_re = jnp.broadcast_to(c_re[j][k : k + 1], (8, WIDE))
+                        r_im = jnp.broadcast_to(c_im[j][k : k + 1], (8, WIDE))
+                        s_re, s_im = r_re * q_re - r_im * q_im, r_re * q_im + r_im * q_re
+                        c_re[j] = jnp.where(pivot, s_re, c_re[j] - (m_re * s_re - m_im * s_im))
+                        c_im[j] = jnp.where(pivot, s_im, c_im[j] - (m_re * s_im + m_im * s_re))
+                    x, z = (
+                        jnp.where(pivot, x_s, x - (m_re * x_s + m_im * z_s)),
+                        jnp.where(pivot, z_s, z - (m_re * z_s - m_im * x_s)),
+                    )
+                for q in blocks:
+                    if q == p:
+                        continue
+                    total = None
+                    for k in range(8):
+                        n_re = jnp.broadcast_to(rows[q][:, 8 * p + k : 8 * p + k + 1], (8, WIDE))
+                        n_im = jnp.broadcast_to(rows[q][:, BS + 8 * p + k : BS + 8 * p + k + 1], (8, WIDE))
+                        term = n_re * x[k : k + 1] + n_im * z[k : k + 1]
+                        total = term if total is None else total + term
+                    rows[q] = jnp.where(own, 0.0, rows[q]) - total
+                rows[p] = x
         for b, m in enumerate(mats):
-            rows = m[8 * p : 8 * p + 8]
-            col_re = [jnp.broadcast_to(m[:, 8 * p + k : 8 * p + k + 1], (BS, WIDE)) for k in range(8)]
-            col_im = [
-                jnp.broadcast_to(m[:, BS + 8 * p + k : BS + 8 * p + k + 1], (BS, WIDE)) for k in range(8)
-            ]
-            x = jnp.where(own, jnp.where(lane8 == row8 + 8 * p, 1.0, 0.0), rows)
-            z = jnp.where(own, jnp.where(lane8 == row8 + (8 * p + BS), 1.0, 0.0), times_i(rows))
-            c_re = [c[8 * p : 8 * p + 8] for c in col_re]
-            c_im = [c[8 * p : 8 * p + 8] for c in col_im]
-            for k in range(8):
-                p_re = jnp.broadcast_to(c_re[k][k : k + 1], (8, WIDE))
-                p_im = jnp.broadcast_to(c_im[k][k : k + 1], (8, WIDE))
-                scale = 1.0 / (p_re * p_re + p_im * p_im)
-                q_re, q_im = p_re * scale, -(p_im * scale)
-                x_k = jnp.broadcast_to(x[k : k + 1], (8, WIDE))
-                z_k = jnp.broadcast_to(z[k : k + 1], (8, WIDE))
-                x_s, z_s = x_k * q_re + z_k * q_im, z_k * q_re - x_k * q_im
-                m_re, m_im = c_re[k], c_im[k]
-                pivot = row8 == k
-                for j in range(k + 1, 8):
-                    r_re = jnp.broadcast_to(c_re[j][k : k + 1], (8, WIDE))
-                    r_im = jnp.broadcast_to(c_im[j][k : k + 1], (8, WIDE))
-                    s_re, s_im = r_re * q_re - r_im * q_im, r_re * q_im + r_im * q_re
-                    c_re[j] = jnp.where(pivot, s_re, c_re[j] - (m_re * s_re - m_im * s_im))
-                    c_im[j] = jnp.where(pivot, s_im, c_im[j] - (m_re * s_im + m_im * s_re))
-                x, z = (
-                    jnp.where(pivot, x_s, x - (m_re * x_s + m_im * z_s)),
-                    jnp.where(pivot, z_s, z - (m_re * z_s - m_im * x_s)),
-                )
-            total = None
-            for k in range(8):
-                term = col_re[k] * x[k : k + 1] + col_im[k] * z[k : k + 1]
-                total = term if total is None else total + term
-            rest = jnp.where(panel, 0.0, m) - total
-            parts = [x if q == p else rest[8 * q : 8 * q + 8] for q in range(BS // 8)]
+            if size == BS:
+                mats[b] = jnp.concatenate([held[b][q] for q in blocks], 0)
+                continue
+            x = jnp.concatenate([held[b][q] for q in blocks], 0)
+            before = jnp.zeros((start, WIDE), f32)
+            after = jnp.zeros((BS - size - start, WIDE), f32)
+            right = [r for r in (before, x, after, before, times_i(x), after) if r.shape[0]]
+            gone = jnp.dot(
+                m, jnp.concatenate(right, 0), precision=lax.Precision.HIGHEST, preferred_element_type=f32
+            )
+            rest = jnp.where(group, 0.0, m) - gone
+            parts = [r for r in (rest[:start], x, rest[start + size :]) if r.shape[0]]
             mats[b] = jnp.concatenate(parts, 0)
     return mats
 
@@ -117,7 +141,11 @@
     while h < n_seg:
         hops.append(h)
         h *= 2
+    far = n_z // 2
+    leap = far // 2 if far >= 4 else n_z
     greeted = [(up_e, s), (down_e, s), (pair_e, s)]
+    if leap < far:
+        greeted += [((e + 2 * leap) % n_energy, s), ((e + n_energy - 2 * leap) % n_energy, s)]
     for h in hops[:-1]:
         greeted += [(e, (s + h) % n_seg), (e, (s + n_seg - h) % n_seg)]
     greeted.append((e, (s + n_seg // 2) % n_seg))
@@ -151,7 +179,7 @@
     many = jnp.full((BS, WIDE), count, jnp.int32)
     has0, has1, has2 = many >= 4, many >= 3, many >= 2
 
-    g0, g2 = inverses([a[0], a[2]])
+    g0, g2 = inverses([a[0], a[2]], BS // 2)
     ((g0w1, g0v0),) = products([g0], [w[1], v[0]])
     ((g2w3, g2v2),) = products([g2], [w[3], v[2]])
     (u01, d0l), (d01, l10) = products([w[0], v[1]], [g0w1, g0v0])
@@ -175,47 +203,50 @@
     keep[2] = l_own
     pl.semaphore_wait(barrier, len(greeted))
 
-    def right_copy(level, h):
+    def right_copy(level, h, part):
+        first, size = ((0, 1), (1, 2))[part]
         return pltpu.make_async_remote_copy(
-            src_ref=outbox.at[level, pl.ds(0, 3)],
-            dst_ref=from_left.at[level],
-            send_sem=right_send.at[level],
-            recv_sem=left_recv.at[level],
+            src_ref=outbox.at[level, pl.ds(first, size)],
+            dst_ref=from_left.at[level, pl.ds(first, size)],
+            send_sem=right_send.at[level, part],
+            recv_sem=left_recv.at[level, part],
             device_id=(e, (s + h) % n_seg),
             device_id_type=MESH,
         )
 
-    def left_copy(level, h):
+    def left_copy(level, h, part):
+        first, size = ((2, 1), (0, 2))[part]
         return pltpu.make_async_remote_copy(
-            src_ref=outbox.at[level, pl.ds(1, 3)],
-            dst_ref=from_right.at[level],
-            send_sem=left_send.at[level],
-            recv_sem=right_recv.at[level],
+            src_ref=outbox.at[level, pl.ds(first + 1, size)],
+            dst_ref=from_right.at[level, pl.ds(first, size)],
+            send_sem=left_send.at[level, part],
+            recv_sem=right_recv.at[level, part],
             device_id=(e, (s + n_seg - h) % n_seg),
             device_id_type=MESH,
         )
 
-    def start_left(level, h):
+    def start_left(level, h, part):
         @pl.when(s >= h)
         def _():
-            left_copy(level, h).start()
-
-    def start_right(level, h):
+            left_copy(level, h, part).start()
+
+    def start_right(level, h, part):
         @pl.when(s + h < n_seg)
         def _():
-            right_copy(level, h).start()
-
-    def await_right(level, h):
+            right_copy(level, h, part).start()
+
+    def await_right(level, h, part):
         @pl.when(s + h < n_seg)
         def _():
-            left_copy(level, h).wait_recv()
-
-    def await_left(level, h):
+            left_copy(level, h, part).wait_recv()
+
+    def await_left(level, h, part):
         @pl.when(s >= h)
         def _():
-            right_copy(level, h).wait_recv()
-
-    start_left(0, 1)
+            right_copy(level, h, part).wait_recv()
+
+    start_left(0, 1, 0)
+    start_left(0, 1, 1)
     here = jnp.full((BS, WIDE), s, jnp.int32)
 
     def interior_factors():
@@ -236,42 +267,50 @@
     state[0] = sigma_left
     state[1] = u_own
     state[2] = l_own
-    await_right(0, 1)
-    joined = here + 1 < n_seg
-    first_right = jnp.where(joined, from_right[0, 2], 0.0)
+    await_right(0, 1, 0)
+    first_right = jnp.where(here + 1 < n_seg, from_right[0, 2], 0.0)
     keep[3] = first_right
-    state[3] = jnp.where(joined, from_right[0, 0], 0.0)
-    state[4] = jnp.where(joined, from_right[0, 1], 0.0)
     state[5] = first_right
 
+    def take_pairs(level, h):
+        if level > 0:
+            await_left(level, h, 1)
+            joined = here >= h
+            state[1] = jnp.where(joined, from_left[level, 1], 0.0)
+            state[2] = jnp.where(joined, from_left[level, 2], 0.0)
+        await_right(level, h, 1)
+        joined = here + h < n_seg
+        state[3] = jnp.where(joined, from_right[level, 0], 0.0)
+        state[4] = jnp.where(joined, from_right[level, 1], 0.0)
+
+    last = (0, 1)
     for level, h in enumerate(hops[:-1], 1):
         (inner,) = inverses([keep[0] - state[0] - state[5]])
+        take_pairs(*last)
+        last = (level, h)
         ((to_r, to_l),) = products([inner], [state[3], state[2]])
-        ((add_r, l_new), (u_new, add_l)) = products([state[4], state[1]], [to_r, to_l])
-        outbox[level, 0] = add_r
-        outbox[level, 1] = u_new
-        outbox[level, 2] = l_new
-        outbox[level, 3] = add_l
-        start_right(level, h)
-        start_left(level, h)
+        wide_r, wide_l = expand(to_r), expand(to_l)
+        outbox[level, 0] = multiply(state[4], wide_r)
+        outbox[level, 3] = multiply(state[1], wide_l)
+        start_right(level, h, 0)
+        start_left(level, h, 0)
+        outbox[level, 1] = multiply(state[1], wide_r)
+        outbox[level, 2] = multiply(state[4], wide_l)
+        start_right(level, h, 1)
+        start_left(level, h, 1)
         if level == 1:
             load.wait()
             for j in range(screened.shape[0]):
                 for k in range(SLOTS):
                     turned[j, k] = pltpu.roll(screened[j, 0, k], BS, 1)
-        await_left(level, h)
-        joined = here >= h
-        state[0] = state[0] + jnp.where(joined, from_left[level, 0], 0.0)
-        state[1] = jnp.where(joined, from_left[level, 1], 0.0)
-        state[2] = jnp.where(joined, from_left[level, 2], 0.0)
-        await_right(level, h)
-        joined = here + h < n_seg
-        state[3] = jnp.where(joined, from_right[level, 0], 0.0)
-        state[4] = jnp.where(joined, from_right[level, 1], 0.0)
-        state[5] = state[5] + jnp.where(joined, from_right[level, 2], 0.0)
+        await_left(level, h, 0)
+        state[0] = state[0] + jnp.where(here >= h, from_left[level, 0], 0.0)
+        await_right(level, h, 0)
+        state[5] = state[5] + jnp.where(here + h < n_seg, from_right[level, 2], 0.0)
 
     lower = here < n_seg // 2
     (inner,) = inverses([keep[0] - state[0] - state[5]])
+    take_pairs(*last)
     near = product(inner, jnp.where(lower, state[3], state[2]))
     half_in[0] = product(jnp.where(lower, state[4], state[1]), near)
     half = pltpu.make_async_remote_copy(
@@ -289,7 +328,7 @@
     sigma_right = state[5] + jnp.where(lower, arrived, 0.0)
 
     g_rep, g_end = inverses(
-        [keep[0] - sigma_left - sigma_right, keep[0] - sigma_left - keep[3]]
+        [keep[0] - sigma_left - sigma_right, keep[0] - sigma_left - keep[3]], BS // 2
     )
     g_out[...] = g_end
     end_copy = pltpu.make_async_remote_copy(
@@ -305,13 +344,15 @@
     def _():
         end_copy.start()
 
-    far = n_z // 2
     pieces = [(SLOTS - 1, 1), (0, SLOTS - 1)]
     split = [(0, 2), (2, 2)]
 
     def ring_copy(way, d, piece):
         first, size = pieces[piece] if d < far else split[way]
-        if way == 0:
+        if d == leap:
+            owner = e
+            target = (e + 2 * leap) % n_energy if way == 0 else (e + n_energy - 2 * leap) % n_energy
+        elif way == 0:
             owner, target = (e + 2 * (n_energy - d + 1)) % n_energy, up_e
         else:
             owner, target = (e + 2 * (d - 1)) % n_energy, down_e
@@ -353,6 +394,9 @@
         )
 
     def start_own(piece):
+        for way in range(2):
+            if leap < far:
+                ring_copy(way, leap, piece).start()
         for way in range(2):
             if far > 1:
                 ring_copy(way, 1, piece).start()
@@ -382,11 +426,16 @@
         for way in range(2):
             ring_copy(way, 1, 0).start()
 
-    for d in range(1, far):
+    order = list(range(1, far))
+    if leap < far:
+        order = sorted(set(range(1, far)), key=lambda d: d + 0.5 if d < leap else d - leap + 1.6)
+    for d in order:
         for piece in range(2):
             for way in range(2):
                 ring_arrival(way, d, piece)
-                if d + 1 < far:
+                if d + 1 == leap:
+                    pass
+                elif d + 1 < far:
                     ring_copy(way, d + 1, piece).start()
                 elif piece == 1:
                     ring_copy(way, far, 0).start()
@@ -409,16 +458,17 @@
         pair_copy(way, d, piece, arriving=True).wait_recv()
 
     for level, h in enumerate([1] + hops[:-1]):
-
-        @pl.when(s >= h)
-        def _(level=level, h=h):
-            left_copy(level, h).wait_send()
-
-        if level > 0:
-
-            @pl.when(s + h < n_seg)
-            def _(level=level, h=h):
-                right_copy(level, h).wait_send()
+        for part in range(2):
+
+            @pl.when(s >= h)
+            def _(level=level, h=h, part=part):
+                left_copy(level, h, part).wait_send()
+
+            if level > 0:
+
+                @pl.when(s + h < n_seg)
+                def _(level=level, h=h, part=part):
+                    right_copy(level, h, part).wait_send()
 
     half.wait_send()
 
@@ -471,10 +521,10 @@
             pltpu.VMEM((shifts, 1, SLOTS) + block, f32),
             pltpu.VMEM((shifts, SLOTS) + block, f32),
             dma,
-            dma((levels,)),
-            dma((levels,)),
-            dma((levels,)),
-            dma((levels,)),
+            dma((levels, 2)),
+            dma((levels, 2)),
+            dma((levels, 2)),
+            dma((levels, 2)),
             dma,
             dma,
             dma,

time: 98 us -> 86.8 us (0.89)
  Pallas kernels: 94.9 us -> 83.7 us
    pallas_call x1, Pallas kernels: 94.9 us -> 83.7 us  [body(): pl.pallas_call(functools.partial(kernel, n_energy, n_seg), out_shape=jax....]
where the time goes in v2:
time: 86.8 us; the launch traced here: 86.6 us
  Pallas kernels  83.7 us (96%)
  local copies, waits for them, and re-layouts  1.57 us (2%)
  between operations  1.31 us (2%)
    pallas_call x1, Pallas kernels, body(): pl.pallas_call(functools.partial(kernel, n_energy, n_seg), out_shape=jax....  83.7 us

profile of v2, /device:TPU:9, one launch (start us, length us, event | category | flops | bytes accessed | tf_op | source)
XLA Modules:
  0.0 86.6 jit_solution(16535456800215757544)
XLA Ops:
  1.3 83.7 %greens.1 = f32[1,1,4,64,128]{4,3,2,1,0:T(8,128)} custom-call(s32[1]{0:T(128)S(6)} %copy.11.counts, s32[1,8]{1,0:T(1,128)} %sources.1, f32[1]{0:T(128)S(6)} %copy.10.energies, f32[1,4,64,128]{3,2,1,0:T(8,128)} %h_ref.1, f32[1,4,64,128]{3,2,1,0:T(8,128)} %u_ref.1, f32[1,1,256]{2,1,0:T(1,128)} %real_ref.1, f32[1,1,256]{2,1,0:T(1,128)} %rate_ref.1, ...), custom_call_target="tpu_custom_call" | custom-call | tf_op jit(solution)/shard_map/greens/pallas_call | solution.py:502
  85.0 1.6 %copy.12 = f32[1,1,4,64,128]{4,3,2,1,0:T(8,128)} copy(f32[1,1,4,64,128]{4,3,2,1,0:T(8,128)} %greens.1) | data formatting | bytes 262144

commit v3 on v2

--- a/solution.py
+++ b/solution.py
@@ -59,12 +59,13 @@
         group = (lane & (BS - 1)) // size == start // size
         blocks = range(start // 8, (start + size) // 8)
         held = [{q: m[8 * q : 8 * q + 8] for q in blocks} for m in mats]
+        also = [{q: times_i(m[8 * q : 8 * q + 8]) for q in blocks} for m in mats]
         for p in blocks:
             own = (lane8 & (BS - 1)) // 8 == p
-            for rows in held:
+            for rows, turned in zip(held, also):
                 mine = rows[p]
                 x = jnp.where(own, jnp.where(lane8 == row8 + 8 * p, 1.0, 0.0), mine)
-                z = jnp.where(own, jnp.where(lane8 == row8 + (8 * p + BS), 1.0, 0.0), times_i(mine))
+                z = jnp.where(own, jnp.where(lane8 == row8 + (8 * p + BS), 1.0, 0.0), turned[p])
                 c_re = [jnp.broadcast_to(mine[:, 8 * p + k : 8 * p + k + 1], (8, WIDE)) for k in range(8)]
                 c_im = [
                     jnp.broadcast_to(mine[:, BS + 8 * p + k : BS + 8 * p + k + 1], (8, WIDE))
@@ -90,16 +91,23 @@
                         jnp.where(pivot, x_s, x - (m_re * x_s + m_im * z_s)),
                         jnp.where(pivot, z_s, z - (m_re * z_s - m_im * x_s)),
                     )
-                for q in blocks:
+                xs = [jnp.broadcast_to(x[k : k + 1], (8, WIDE)) for k in range(8)]
+                zs = [jnp.broadcast_to(z[k : k + 1], (8, WIDE)) for k in range(8)]
+                for q in sorted(blocks, key=lambda q: (q - p) % 8):
                     if q == p:
                         continue
-                    total = None
+                    terms = [jnp.where(own, 0.0, rows[q])]
+                    others = [jnp.where(own, 0.0, turned[q])]
                     for k in range(8):
                         n_re = jnp.broadcast_to(rows[q][:, 8 * p + k : 8 * p + k + 1], (8, WIDE))
                         n_im = jnp.broadcast_to(rows[q][:, BS + 8 * p + k : BS + 8 * p + k + 1], (8, WIDE))
-                        term = n_re * x[k : k + 1] + n_im * z[k : k + 1]
-                        total = term if total is None else total + term
-                    rows[q] = jnp.where(own, 0.0, rows[q]) - total
+                        terms.append(-(n_re * xs[k] + n_im * zs[k]))
+                        others.append(n_im * xs[k] - n_re * zs[k])
+                    while len(terms) > 1:
+                        terms = [sum(terms[n + 1 : n + 2], terms[n]) for n in range(0, len(terms), 2)]
+                    while len(others) > 1:
+                        others = [sum(others[n + 1 : n + 2], others[n]) for n in range(0, len(others), 2)]
+                    rows[q], turned[q] = terms[0], others[0]
                 rows[p] = x
         for b, m in enumerate(mats):
             if size == BS:
@@ -142,7 +150,7 @@
         hops.append(h)
         h *= 2
     far = n_z // 2
-    leap = far // 2 if far >= 4 else n_z
+    leap = far // 2 + 1 if far >= 4 else n_z
     greeted = [(up_e, s), (down_e, s), (pair_e, s)]
     if leap < far:
         greeted += [((e + 2 * leap) % n_energy, s), ((e + n_energy - 2 * leap) % n_energy, s)]

time: 86.8 us -> 82.8 us (0.954)
  Pallas kernels: 83.7 us -> 79.8 us
    pallas_call x1, Pallas kernels: 83.7 us -> 79.8 us  [body(): pl.pallas_call(functools.partial(kernel, n_energy, n_seg), out_shape=jax....]
where the time goes in v3:
time: 82.8 us; the launch traced here: 82.6 us
  Pallas kernels  79.8 us (96%)
  local copies, waits for them, and re-layouts  1.57 us (2%)
  between operations  1.31 us (2%)
    pallas_call x1, Pallas kernels, body(): pl.pallas_call(functools.partial(kernel, n_energy, n_seg), out_shape=jax....  79.8 us

profile of v3, /device:TPU:9, one launch (start us, length us, event | category | flops | bytes accessed | tf_op | source)
XLA Modules:
  0.0 82.6 jit_solution(5919854087334194375)
XLA Ops:
  1.3 79.8 %greens.1 = f32[1,1,4,64,128]{4,3,2,1,0:T(8,128)} custom-call(s32[1]{0:T(128)S(6)} %copy.11.counts, s32[1,8]{1,0:T(1,128)} %sources.1, f32[1]{0:T(128)S(6)} %copy.10.energies, f32[1,4,64,128]{3,2,1,0:T(8,128)} %h_ref.1, f32[1,4,64,128]{3,2,1,0:T(8,128)} %u_ref.1, f32[1,1,256]{2,1,0:T(1,128)} %real_ref.1, f32[1,1,256]{2,1,0:T(1,128)} %rate_ref.1, ...), custom_call_target="tpu_custom_call" | custom-call | tf_op jit(solution)/shard_map/greens/pallas_call | solution.py:510
  81.1 1.6 %copy.12 = f32[1,1,4,64,128]{4,3,2,1,0:T(8,128)} copy(f32[1,1,4,64,128]{4,3,2,1,0:T(8,128)} %greens.1) | data formatting | bytes 262144
